TPU v7x, 32 devices: a whole 2x2x4 slice. The times are simulated.
32 devices in a mesh: rep: 4 (over y, x), seq: 8 (over z, core).
Axes of the slice: x: 2, y: 2, z: 4, core: 2. Of those that a mesh axis runs over, the one named last changes fastest.
Arguments:
- inputs: bfloat16 [4, 2048, 1536], P('rep', 'seq'), may hold values from -13 to 13
- segment_ids: int32 [4, 2048], P('rep'), may hold values from 0 to 7, as said below
- valid_mask: int32 [4, 2048], P('rep'), may hold values from 0 to 1, as said below
- input_weight: bfloat16 [1536, 4608], P('seq'), may hold values from -0.15625 to 0.15625
- output_weight: bfloat16 [1536, 1536], P('seq'), may hold values from -0.15625 to 0.15625
- conv_kernel: float32 [16, 6, 11], replicated, may hold values from -1.2 to 1.2
- head_mix: float32 [8, 2, 2], replicated, may hold values from 0.2 to 1
- first_gain: float32 [1536], replicated, may hold values from 0.5 to 1.5
- second_gain: float32 [1536], replicated, may hold values from 0.5 to 1.5
- group_gain: float32 [1536], replicated, may hold values from 0.5 to 1.5
- gate_weight: bfloat16 [1536, 4096], P(None, 'seq'), may hold values from -0.15625 to 0.15625
- up_weight: bfloat16 [1536, 4096], P(None, 'seq'), may hold values from -0.15625 to 0.15625
- down_weight: bfloat16 [4096, 1536], P('seq'), may hold values from -0.09375 to 0.09375
- cotangent: bfloat16 [4, 2048, 1536], P('rep', 'seq'), may hold values from -17 to 17
Outputs:
- output: bfloat16 [4, 2048, 1536], P('rep', 'seq')
- grad_inputs: bfloat16 [4, 2048, 1536], P('rep', 'seq')
- grad_input_weight: float32 [1536, 4608], P('seq')
- grad_output_weight: float32 [1536, 1536], P('seq')
- grad_kernel: float32 [16, 6, 11], replicated
- grad_mix: float32 [8, 2, 2], replicated
- grad_first_gain: float32 [1536], replicated
- grad_second_gain: float32 [1536], replicated
- grad_group_gain: float32 [1536], replicated
- grad_gate: float32 [1536, 4096], P(None, 'seq')
- grad_up: float32 [1536, 4096], P(None, 'seq')
- grad_down: float32 [4096, 1536], P('seq')
Inputs may be any that keep to these rules, and one draw needn't show every extreme that they name: `segment_ids`: segment ids never fall along a sequence and start at 0. The positions k * 1024 to (k + 1) * 1024 - 1 form frame k; every document lies inside one frame, a frame holds one to four documents, the first frame of the first sequence is a single document of exactly 1024 positions, and every frame of the last sequence holds four documents. `valid_mask`: in each frame the positions with 0 form its tail, at most 256 of them; the first frame of the first sequence has none.
All inputs are finite; a program needn't handle non-finite values.
Results may differ from a plain program's by a relative error of at most 0.02.
Values may be sent and summed in bfloat16 or wider, within the bound.
A program may use at most 384 MiB of HBM per device.

v0:
```python
import jax
import jax.numpy as jnp
from jax import lax
from jax.sharding import PartitionSpec as P

REACH = 4
EPS = 1e-06
HIGHEST = lax.Precision.HIGHEST


def from_behind(x, axis, by):
    count = lax.axis_size(axis)
    pairs = [(i, i + by) for i in range(count) if 0 <= i + by < count]
    return lax.ppermute(x, axis, pairs)


def convolve(logits, kernel, rows, columns):
    rim_rows = kernel.shape[1] - 1
    key_span = kernel.shape[2] - 1
    result = jnp.zeros((logits.shape[0], rows, columns), jnp.float32)
    for row_tap in range(kernel.shape[1]):
        for col_tap in range(kernel.shape[2]):
            weight = kernel[:, row_tap, col_tap][:, None, None]
            result = (
                result
                + weight
                * logits[
                    :,
                    rim_rows - row_tap : rim_rows - row_tap + rows,
                    key_span - col_tap : key_span - col_tap + columns,
                ]
            )
    return result


def convolve_back(grads, kernel):
    rim_rows = kernel.shape[1] - 1
    key_span = kernel.shape[2] - 1
    rows = grads.shape[1] + rim_rows
    columns = grads.shape[2] + key_span
    padded = jnp.pad(grads, ((0, 0), (rim_rows, rim_rows), (key_span, key_span)))
    result = jnp.zeros((grads.shape[0], rows, columns), jnp.float32)
    for row_tap in range(kernel.shape[1]):
        for col_tap in range(kernel.shape[2]):
            weight = kernel[:, row_tap, col_tap][:, None, None]
            result = (
                result + weight * padded[:, row_tap : row_tap + rows, col_tap : col_tap + columns]
            )
    return result


def kernel_grads(grads, logits, taps_rows, taps_cols):
    rim_rows = taps_rows - 1
    key_span = taps_cols - 1
    rows = grads.shape[1]
    columns = grads.shape[2]
    entries = []
    for row_tap in range(taps_rows):
        line_sums = []
        for col_tap in range(taps_cols):
            window_part = logits[
                :,
                rim_rows - row_tap : rim_rows - row_tap + rows,
                key_span - col_tap : key_span - col_tap + columns,
            ]
            line_sums.append(jnp.sum(grads * window_part, axis=(1, 2)))
        entries.append(jnp.stack(line_sums, axis=-1))
    return jnp.stack(entries, axis=1)


def attend_group(operands, mask_ext, mask_own, row_valid, score_scale):
    query_g, key_g, value_g, kernel_g, mixing_g = operands
    rows = mask_own.shape[0]
    columns = mask_own.shape[1]
    raw = jnp.einsum("qhd,khd->hqk", query_g, key_g, preferred_element_type=jnp.float32)
    logits = raw * score_scale * mask_ext
    conv = convolve(logits, kernel_g, rows, columns)
    allowed = mask_own > 0
    peak = jnp.max(jnp.where(allowed, conv, -1e30), axis=-1, keepdims=True)
    peak = jnp.where(row_valid > 0, peak, 0.0)
    expo = jnp.where(allowed, jnp.exp(conv - peak), 0.0)
    denom = jnp.sum(expo, axis=-1, keepdims=True) + 1.0 - row_valid
    prob = expo / denom
    mixed = (
        mixing_g[:, 0][:, None, None] * prob[0][None]
        + mixing_g[:, 1][:, None, None] * prob[1][None]
    )
    mixed_low = mixed.astype(jnp.bfloat16)
    result = jnp.einsum("hqk,khd->qhd", mixed_low, value_g, preferred_element_type=jnp.float32)
    return (result, peak + jnp.log(denom))


def attend_group_back(operands, mask_ext, mask_own, score_scale):
    query_g, key_g, value_g, kernel_g, mixing_g, dresult_g, lse_g = operands
    rows = mask_own.shape[0]
    columns = mask_own.shape[1]
    raw = jnp.einsum("qhd,khd->hqk", query_g, key_g, preferred_element_type=jnp.float32)
    logits = raw * score_scale * mask_ext
    conv = convolve(logits, kernel_g, rows, columns)
    allowed = mask_own > 0
    prob = jnp.where(allowed, jnp.exp(conv - lse_g), 0.0)
    mixed = (
        mixing_g[:, 0][:, None, None] * prob[0][None]
        + mixing_g[:, 1][:, None, None] * prob[1][None]
    )
    mixed_low = mixed.astype(jnp.bfloat16)
    dmixed = jnp.einsum("qhd,khd->hqk", dresult_g, value_g, preferred_element_type=jnp.float32)
    dvalue = jnp.einsum("hqk,qhd->khd", mixed_low, dresult_g, preferred_element_type=jnp.float32)
    dmixing = jnp.stack(
        [
            jnp.sum(dmixed * prob[0][None], axis=(1, 2)),
            jnp.sum(dmixed * prob[1][None], axis=(1, 2)),
        ],
        axis=-1,
    )
    dprob = (
        mixing_g[0][:, None, None] * dmixed[0][None] + mixing_g[1][:, None, None] * dmixed[1][None]
    )
    dconv = prob * (dprob - jnp.sum(prob * dprob, axis=-1, keepdims=True))
    dkernel = kernel_grads(dconv, logits, kernel_g.shape[1], kernel_g.shape[2])
    dlogits = convolve_back(dconv, kernel_g) * mask_ext * score_scale
    dquery = jnp.einsum(
        "hqk,khd->qhd",
        dlogits,
        key_g.astype(jnp.float32),
        precision=HIGHEST,
        preferred_element_type=jnp.float32,
    )
    dkey = jnp.einsum(
        "hqk,qhd->khd",
        dlogits,
        query_g.astype(jnp.float32),
        precision=HIGHEST,
        preferred_element_type=jnp.float32,
    )
    return (dquery, dkey, dvalue, dkernel, dmixing)


def rms_scale(values):
    return lax.rsqrt(jnp.mean(values * values, axis=-1, keepdims=True) + EPS)


def norm_back(grad_out, values, inv_scale, gain):
    scaled_grad = grad_out * gain
    inner = jnp.mean(scaled_grad * values, axis=-1, keepdims=True)
    return inv_scale * scaled_grad - values * inv_scale**3 * inner


def on_device(
    inputs,
    segment_ids,
    valid_mask,
    input_weight,
    output_weight,
    conv_kernel,
    head_mix,
    first_gain,
    second_gain,
    group_gain,
    gate_weight,
    up_weight,
    down_weight,
    cotangent,
):
    tokens = inputs.shape[1]
    model_width = inputs.shape[2]
    head_count = conv_kernel.shape[0]
    head_dim = model_width // head_count
    groups = head_mix.shape[0]
    rim_rows = conv_kernel.shape[1] - 1
    half_span = conv_kernel.shape[2] // 2
    window = REACH * tokens
    score_scale = head_dim ** (-0.5)
    seq_rank = lax.axis_index("seq")
    row_start = seq_rank * tokens
    window_start = row_start - (REACH - 1) * tokens
    resid_in = inputs[0].astype(jnp.float32)
    grad_out = cotangent[0].astype(jnp.float32)
    offset = window + half_span
    segment_pad = jnp.concatenate(
        [jnp.full((offset,), -1, jnp.int32), segment_ids[0], jnp.full((half_span,), -1, jnp.int32)]
    )
    valid_pad = jnp.concatenate(
        [jnp.zeros((offset,), jnp.int32), valid_mask[0], jnp.zeros((half_span,), jnp.int32)]
    )
    query_pos = row_start - rim_rows + jnp.arange(tokens + rim_rows, dtype=jnp.int32)
    key_pos = window_start - half_span + jnp.arange(window + 2 * half_span, dtype=jnp.int32)
    query_seg = lax.dynamic_slice_in_dim(
        segment_pad, row_start - rim_rows + offset, tokens + rim_rows
    )
    key_seg = lax.dynamic_slice_in_dim(
        segment_pad, window_start - half_span + offset, window + 2 * half_span
    )
    query_live = lax.dynamic_slice_in_dim(
        valid_pad, row_start - rim_rows + offset, tokens + rim_rows
    )
    key_live = lax.dynamic_slice_in_dim(
        valid_pad, window_start - half_span + offset, window + 2 * half_span
    )
    mask_ext = (
        (query_seg[:, None] == key_seg[None, :])
        & (key_pos[None, :] <= query_pos[:, None])
        & (query_live[:, None] > 0)
        & (key_live[None, :] > 0)
    ).astype(jnp.float32)
    mask_own = mask_ext[rim_rows:, half_span : half_span + window]
    row_valid = query_live[rim_rows:].astype(jnp.float32)[:, None]
    full_input, full_output = (
        lax.all_gather(input_weight, "seq", axis=0, tiled=True),
        lax.all_gather(output_weight, "seq", axis=0, tiled=True),
    )
    first_scale = rms_scale(resid_in)
    normed_in = (resid_in * first_scale * first_gain).astype(jnp.bfloat16)
    projected = jnp.dot(normed_in, full_input, preferred_element_type=jnp.float32).astype(
        jnp.bfloat16
    )
    query = projected[:, :model_width]
    keys_values = projected[:, model_width:]
    query_rim = from_behind(query[tokens - rim_rows :], "seq", 1)
    query_ext = jnp.concatenate([query_rim, query], axis=0)
    pieces = [keys_values]
    for distance in range(1, REACH):
        pieces.append(from_behind(keys_values, "seq", distance))
    window_rows = jnp.concatenate(pieces[::-1], axis=0)
    key_ext = jnp.pad(window_rows[:, :model_width], ((half_span, half_span), (0, 0)))
    value_window = window_rows[:, model_width:]

    def split_heads(values):
        return values.reshape(values.shape[0], groups, 2, head_dim).transpose(1, 0, 2, 3)

    def merge_heads(values):
        return values.transpose(1, 0, 2, 3).reshape(values.shape[1], model_width)

    query_groups = split_heads(query_ext)
    key_groups = split_heads(key_ext)
    value_groups = split_heads(value_window)
    kernel_groups = conv_kernel.reshape(groups, 2, conv_kernel.shape[1], conv_kernel.shape[2])
    result_groups, lse_groups = lax.map(
        lambda operands: attend_group(operands, mask_ext, mask_own, row_valid, score_scale),
        (query_groups, key_groups, value_groups, kernel_groups, head_mix),
    )
    attended = merge_heads(result_groups)
    shaped = attended.reshape(tokens, head_count, head_dim)
    centred = shaped - jnp.mean(shaped, axis=-1, keepdims=True)
    inv_std = lax.rsqrt(jnp.mean(centred * centred, axis=-1, keepdims=True) + EPS)
    unit_heads = centred * inv_std
    unit = unit_heads.reshape(tokens, model_width)
    normed = (unit * group_gain).astype(jnp.bfloat16)
    branch = jnp.dot(normed, full_output, preferred_element_type=jnp.float32)
    resid = resid_in + row_valid * branch
    second_scale = rms_scale(resid)
    normed_mid = (resid * second_scale * second_gain).astype(jnp.bfloat16)
    dmlp = (row_valid * grad_out).astype(jnp.bfloat16)
    contract_rows = (((0,), (0,)), ((), ()))
    inputs_all = lax.all_gather(normed_mid, "seq", axis=0, tiled=True)
    gate = jnp.dot(inputs_all, gate_weight, preferred_element_type=jnp.float32)
    up_proj = jnp.dot(inputs_all, up_weight, preferred_element_type=jnp.float32)
    hidden = (jax.nn.silu(gate) * up_proj).astype(jnp.bfloat16)
    mlp = lax.psum_scatter(
        jnp.dot(hidden, down_weight, preferred_element_type=jnp.float32).astype(jnp.bfloat16),
        "seq",
        scatter_dimension=0,
        tiled=True,
    ).astype(jnp.float32)
    result = resid + row_valid * mlp
    dmlp_all = lax.all_gather(dmlp, "seq", axis=0, tiled=True)
    dhidden = jnp.dot(dmlp_all, down_weight.T, preferred_element_type=jnp.float32)
    sigmoid_gate = jax.nn.sigmoid(gate)
    gate_grad = (dhidden * up_proj * sigmoid_gate * (1.0 + gate * (1.0 - sigmoid_gate))).astype(
        jnp.bfloat16
    )
    up_grad = (dhidden * gate * sigmoid_gate).astype(jnp.bfloat16)
    grad_down = lax.dot_general(hidden, dmlp_all, contract_rows, preferred_element_type=jnp.float32)
    grad_gate = lax.dot_general(
        inputs_all, gate_grad, contract_rows, preferred_element_type=jnp.float32
    )
    grad_up = lax.dot_general(
        inputs_all, up_grad, contract_rows, preferred_element_type=jnp.float32
    )
    dmid = lax.psum_scatter(
        (
            jnp.dot(gate_grad, gate_weight.T, preferred_element_type=jnp.float32)
            + jnp.dot(up_grad, up_weight.T, preferred_element_type=jnp.float32)
        ).astype(jnp.bfloat16),
        "seq",
        scatter_dimension=0,
        tiled=True,
    ).astype(jnp.float32)
    second_part = jnp.sum(dmid * resid * second_scale, axis=0)
    dresid = grad_out + norm_back(dmid, resid, second_scale, second_gain)
    dbranch = (row_valid * dresid).astype(jnp.bfloat16)
    whole_output_grad = lax.dot_general(
        normed, dbranch, contract_rows, preferred_element_type=jnp.float32
    )
    dnormed = jnp.dot(dbranch, full_output.T, preferred_element_type=jnp.float32)
    group_part = jnp.sum(dnormed * unit, axis=0)
    dunit = (dnormed * group_gain).reshape(tokens, head_count, head_dim)
    dshaped = inv_std * (
        dunit
        - jnp.mean(dunit, axis=-1, keepdims=True)
        - unit_heads * jnp.mean(dunit * unit_heads, axis=-1, keepdims=True)
    )
    dattended = dshaped.reshape(tokens, model_width).astype(jnp.bfloat16)
    dquery_g, dkey_g, dvalue_g, dkernel_g, dmixing = lax.map(
        lambda operands: attend_group_back(operands, mask_ext, mask_own, score_scale),
        (
            query_groups,
            key_groups,
            value_groups,
            kernel_groups,
            head_mix,
            split_heads(dattended),
            lse_groups,
        ),
    )
    dquery_ext = merge_heads(dquery_g)
    dkey_window = merge_heads(dkey_g)[half_span : half_span + window]
    dvalue_window = merge_heads(dvalue_g)
    dpair_window = jnp.concatenate([dkey_window, dvalue_window], axis=1)
    dpair = dpair_window[(REACH - 1) * tokens :]
    for distance in range(1, REACH):
        block_first = (REACH - 1 - distance) * tokens
        dpair = dpair + from_behind(
            dpair_window[block_first : block_first + tokens].astype(jnp.bfloat16), "seq", -distance
        ).astype(jnp.float32)
    rim_grad = from_behind(dquery_ext[:rim_rows], "seq", -1)
    dquery_own = dquery_ext[rim_rows:]
    dquery_own = jnp.concatenate(
        [dquery_own[: tokens - rim_rows], dquery_own[tokens - rim_rows :] + rim_grad], axis=0
    )
    dprojected = jnp.concatenate([dquery_own, dpair], axis=1).astype(jnp.bfloat16)
    whole_input_grad = lax.dot_general(
        normed_in, dprojected, contract_rows, preferred_element_type=jnp.float32
    )
    dnormin = jnp.dot(dprojected, full_input.T, preferred_element_type=jnp.float32)
    first_part = jnp.sum(dnormin * resid_in * first_scale, axis=0)
    grad_in = dresid + norm_back(dnormin, resid_in, first_scale, first_gain)
    input_shard, output_shard = (
        lax.psum_scatter(
            whole_input_grad.astype(jnp.bfloat16), "seq", scatter_dimension=0, tiled=True
        ).astype(jnp.float32),
        lax.psum_scatter(
            whole_output_grad.astype(jnp.bfloat16), "seq", scatter_dimension=0, tiled=True
        ).astype(jnp.float32),
    )
    kernel_part = dkernel_g.reshape(head_count, conv_kernel.shape[1], conv_kernel.shape[2])
    grad_kernel, grad_mix, grad_first, grad_second, grad_group = lax.psum(
        (kernel_part, dmixing, first_part, second_part, group_part), ("rep", "seq")
    )
    grad_input_w, grad_output_w, grad_gate, grad_up, grad_down = (
        lax.psum(input_shard.astype(jnp.bfloat16), "rep").astype(jnp.float32),
        lax.psum(output_shard.astype(jnp.bfloat16), "rep").astype(jnp.float32),
        lax.psum(grad_gate.astype(jnp.bfloat16), "rep").astype(jnp.float32),
        lax.psum(grad_up.astype(jnp.bfloat16), "rep").astype(jnp.float32),
        lax.psum(grad_down.astype(jnp.bfloat16), "rep").astype(jnp.float32),
    )
    return (
        result.astype(jnp.bfloat16)[None],
        grad_in.astype(jnp.bfloat16)[None],
        grad_input_w,
        grad_output_w,
        grad_kernel,
        grad_mix,
        grad_first,
        grad_second,
        grad_group,
        grad_gate,
        grad_up,
        grad_down,
    )


def solution(mesh):
    in_specs = (
        P("rep", "seq", None),
        P("rep", None),
        P("rep", None),
        P("seq", None),
        P("seq", None),
        P(),
        P(),
        P(),
        P(),
        P(),
        P(None, "seq"),
        P(None, "seq"),
        P("seq", None),
        P("rep", "seq", None),
    )
    out_specs = (
        P("rep", "seq", None),
        P("rep", "seq", None),
        P("seq", None),
        P("seq", None),
        P(),
        P(),
        P(),
        P(),
        P(),
        P(None, "seq"),
        P(None, "seq"),
        P("seq", None),
    )
    return jax.shard_map(
        on_device, mesh=mesh, in_specs=in_specs, out_specs=out_specs, check_vma=False
    )
```

profile of v0, /device:TPU:0, one launch (start us, length us, event | category | flops | bytes accessed | tf_op | source)
XLA Modules:
  0.0 4016.5 jit_solution(8021908718773649853)
XLA Ops:
  9.3 132.8 %all-gather.5.cloned.1.call-done = bf16[1536,4608]{1,0:T(8,128)(2,1)} async-done(((bf16[192,4608]{1,0:T(8,128)(2,1)}), bf16[1536,4608]{1,0:T(8,128)(2,1)}) %all-gather.5.cloned.1.call-update) | async-done | bytes 14155792 | tf_op jit(solution)/shard_map/all_gather | solution.py:209
  178.6 39.8 collective-permute-done.1
  218.4 47.0 %collective-permute-done = bf16[256,3072]{1,0:T(8,128)(2,1)} collective-permute-done((bf16[256,3072]{1,0:T(8,128)(2,1)}, bf16[256,3072]{1,0:T(8,128)(2,1)}, u32[]{:S(2)}, u32[]{:S(2)}) %collective-permute-start) | collective-permute-done | bytes 1572896 | tf_op jit(solution)/shard_map/ppermute | solution.py:14
  286.9 341.3 %while.34 = (s32[]{:T(128)}, f32[8,256,2,96]{1,3,2,0:T(8,128)S(1)}, f32[8,2,256,1]{2,1,3,0:T(2,128)}, bf16[8,1024,2,96]{1,3,2,0:T(8,128)(2,1)}, f32[8,2,2]{2,1,0...) while((s32[]{:T(128)}, f32[8,256,2,96]{1,3,2,0:T(8,128)S(1)}, ...), condition=%wide.region_4.5_spmd.clone, body=%wide.region_1.4_spmd.clone.sunk | while | flops 281692032 | bytes 160720624 | solution.py:238
  291.5 34.6 select_reduce_fusion.2
  419.5 34.6 select_reduce_fusion.2
  462.1 34.6 select_reduce_fusion.2
  652.1 102.0 %all-gather.9.cloned.1.call-done = bf16[2048,1536]{1,0:T(8,128)(2,1)} async-done(((bf16[256,1536]{1,0:T(8,128)(2,1)}), bf16[2048,1536]{1,0:T(8,128)(2,1)}) %all-gather.9.cloned.1.call-update) | async-done | bytes 6291472 | tf_op jit(solution)/shard_map/all_gather | solution.py:255
  767.9 51.8 %all-gather.11.cloned.1.call-done = bf16[2048,1536]{1,0:T(8,128)(2,1)} async-done(((bf16[256,1536]{1,0:T(8,128)(2,1)}), bf16[2048,1536]{1,0:T(8,128)(2,1)}) %all-gather.11.cloned.1.call-update) | async-done | bytes 6291472 | tf_op jit(solution)/shard_map/all_gather | solution.py:266
  848.9 61.1 %reduce-scatter.7.cloned.1.call-done = bf16[256,1536]{1,0:T(8,128)(2,1)} async-done(((bf16[2048,1536]{1,0:T(8,128)(2,1)}), bf16[256,1536]{1,0:T(8,128)(2,1)}) %reduce-scatter.7.cloned.1.call-update) | async-done | bytes 786448 | tf_op jit(solution)/shard_map/reduce_scatter | solution.py:280
  912.2 68.2 %reduce-scatter.5.cloned.1.call-done = bf16[256,1536]{1,0:T(8,128)(2,1)} async-done(((bf16[2048,1536]{1,0:T(8,128)(2,1)}), bf16[256,1536]{1,0:T(8,128)(2,1)}) %reduce-scatter.5.cloned.1.call-update) | async-done | bytes 786448 | tf_op jit(solution)/shard_map/reduce_scatter | solution.py:259
  1008.2 2550.7 %while.35 = (s32[]{:T(128)}, f32[8,261,2,96]{3,1,2,0:T(8,128)}, f32[8,1034,2,96]{1,3,2,0:T(8,128)}, f32[8,1024,2,96]{1,3,2,0:T(8,128)}, f32[8,2,6,11]{3,1,0,2:T(...) while((s32[]{:T(128)}, f32[8,261,2,96]{3,1,2,0:T(8,128)}, ...), condition=%wide.region_83.84_spmd.clone, body=%wide.region_13.83_spmd.clone.sunk | while | flops 1772737280 | bytes 370601792 | solution.py:304
  1041.3 36.7 multiply_reduce_fusion.77
  1163.3 124.6 %multiply_multiply_fusion.4 = f32[2,261,1034]{2,1,0:T(8,128)S(1)} fusion(f32[2,256,1024]{2,1,0:T(8,128)} %get-tuple-element.1464, f32[261,1034]{1,0:T(8,128)} %fusion.360, f32[2]{0:T(128)} %get-tuple-element.1396, f32[2]{0:T(128)} %get-tuple-element.1397, f32[2]{0:T(128)} %get-tuple-element.1398, f32[2]{0:T(128)} %get-tuple-element.1399, ...), kind=kLoop, calls=%fused_computation.436.clone.1 | loop fusion | flops 71786448 | bytes 5336168 | tf_op jit(solution)/shard_map/while/body/eval_jaxpr/mul | solution.py:121
  1356.6 36.7 multiply_reduce_fusion.77
  1478.6 124.6 %multiply_multiply_fusion.4 = f32[2,261,1034]{2,1,0:T(8,128)S(1)} fusion(f32[2,256,1024]{2,1,0:T(8,128)} %get-tuple-element.1464, f32[261,1034]{1,0:T(8,128)} %fusion.360, f32[2]{0:T(128)} %get-tuple-element.1396, f32[2]{0:T(128)} %get-tuple-element.1397, f32[2]{0:T(128)} %get-tuple-element.1398, f32[2]{0:T(128)} %get-tuple-element.1399, ...), kind=kLoop, calls=%fused_computation.436.clone.1 | loop fusion | flops 71786448 | bytes 5336168 | tf_op jit(solution)/shard_map/while/body/eval_jaxpr/mul | solution.py:121
  1671.8 36.7 multiply_reduce_fusion.77
  1793.8 124.6 %multiply_multiply_fusion.4 = f32[2,261,1034]{2,1,0:T(8,128)S(1)} fusion(f32[2,256,1024]{2,1,0:T(8,128)} %get-tuple-element.1464, f32[261,1034]{1,0:T(8,128)} %fusion.360, f32[2]{0:T(128)} %get-tuple-element.1396, f32[2]{0:T(128)} %get-tuple-element.1397, f32[2]{0:T(128)} %get-tuple-element.1398, f32[2]{0:T(128)} %get-tuple-element.1399, ...), kind=kLoop, calls=%fused_computation.436.clone.1 | loop fusion | flops 71786448 | bytes 5336168 | tf_op jit(solution)/shard_map/while/body/eval_jaxpr/mul | solution.py:121
  1987.1 36.7 multiply_reduce_fusion.77
  2109.1 124.6 %multiply_multiply_fusion.4 = f32[2,261,1034]{2,1,0:T(8,128)S(1)} fusion(f32[2,256,1024]{2,1,0:T(8,128)} %get-tuple-element.1464, f32[261,1034]{1,0:T(8,128)} %fusion.360, f32[2]{0:T(128)} %get-tuple-element.1396, f32[2]{0:T(128)} %get-tuple-element.1397, f32[2]{0:T(128)} %get-tuple-element.1398, f32[2]{0:T(128)} %get-tuple-element.1399, ...), kind=kLoop, calls=%fused_computation.436.clone.1 | loop fusion | flops 71786448 | bytes 5336168 | tf_op jit(solution)/shard_map/while/body/eval_jaxpr/mul | solution.py:121
  2302.4 36.7 multiply_reduce_fusion.77
  2424.4 124.6 %multiply_multiply_fusion.4 = f32[2,261,1034]{2,1,0:T(8,128)S(1)} fusion(f32[2,256,1024]{2,1,0:T(8,128)} %get-tuple-element.1464, f32[261,1034]{1,0:T(8,128)} %fusion.360, f32[2]{0:T(128)} %get-tuple-element.1396, f32[2]{0:T(128)} %get-tuple-element.1397, f32[2]{0:T(128)} %get-tuple-element.1398, f32[2]{0:T(128)} %get-tuple-element.1399, ...), kind=kLoop, calls=%fused_computation.436.clone.1 | loop fusion | flops 71786448 | bytes 5336168 | tf_op jit(solution)/shard_map/while/body/eval_jaxpr/mul | solution.py:121
  2617.6 36.7 multiply_reduce_fusion.77
  2739.6 124.6 %multiply_multiply_fusion.4 = f32[2,261,1034]{2,1,0:T(8,128)S(1)} fusion(f32[2,256,1024]{2,1,0:T(8,128)} %get-tuple-element.1464, f32[261,1034]{1,0:T(8,128)} %fusion.360, f32[2]{0:T(128)} %get-tuple-element.1396, f32[2]{0:T(128)} %get-tuple-element.1397, f32[2]{0:T(128)} %get-tuple-element.1398, f32[2]{0:T(128)} %get-tuple-element.1399, ...), kind=kLoop, calls=%fused_computation.436.clone.1 | loop fusion | flops 71786448 | bytes 5336168 | tf_op jit(solution)/shard_map/while/body/eval_jaxpr/mul | solution.py:121
  2932.9 36.7 multiply_reduce_fusion.77
  3054.9 124.6 %multiply_multiply_fusion.4 = f32[2,261,1034]{2,1,0:T(8,128)S(1)} fusion(f32[2,256,1024]{2,1,0:T(8,128)} %get-tuple-element.1464, f32[261,1034]{1,0:T(8,128)} %fusion.360, f32[2]{0:T(128)} %get-tuple-element.1396, f32[2]{0:T(128)} %get-tuple-element.1397, f32[2]{0:T(128)} %get-tuple-element.1398, f32[2]{0:T(128)} %get-tuple-element.1399, ...), kind=kLoop, calls=%fused_computation.436.clone.1 | loop fusion | flops 71786448 | bytes 5336168 | tf_op jit(solution)/shard_map/while/body/eval_jaxpr/mul | solution.py:121
  3248.2 36.7 multiply_reduce_fusion.77
  3370.2 124.6 %multiply_multiply_fusion.4 = f32[2,261,1034]{2,1,0:T(8,128)S(1)} fusion(f32[2,256,1024]{2,1,0:T(8,128)} %get-tuple-element.1464, f32[261,1034]{1,0:T(8,128)} %fusion.360, f32[2]{0:T(128)} %get-tuple-element.1396, f32[2]{0:T(128)} %get-tuple-element.1397, f32[2]{0:T(128)} %get-tuple-element.1398, f32[2]{0:T(128)} %get-tuple-element.1399, ...), kind=kLoop, calls=%fused_computation.436.clone.1 | loop fusion | flops 71786448 | bytes 5336168 | tf_op jit(solution)/shard_map/while/body/eval_jaxpr/mul | solution.py:121
  3620.5 38.8 collective-permute-done.6
  3693.2 147.7 %reduce-scatter.9.cloned.1.call-done = bf16[192,4608]{1,0:T(8,128)(2,1)} async-done(((bf16[1536,4608]{1,0:T(8,128)(2,1)}), bf16[192,4608]{1,0:T(8,128)(2,1)}) %reduce-scatter.9.cloned.1.call-update) | async-done | bytes 1769488 | tf_op jit(solution)/shard_map/reduce_scatter | solution.py:339
  3853.7 40.1 all-reduce.2
  3898.0 100.9 %all-reduce.6.cloned.1.call-done = (bf16[192,4608]{1,0:T(8,128)(2,1)}, bf16[192,1536]{1,0:T(8,128)(2,1)}, bf16[1536,512]{1,0:T(8,128)(2,1)}, bf16[1536,512]{1,0:T(8,128)(2,1)}, bf16[512,1536]{1,0:T(8,128)(2,1)}) async-done(((bf16[192,4608]{1,0:T(8,128)(2,1)}, bf16[192,1536]{1,0:T(8,128)(2,1)}, bf16[1536,512]{1,0:T(8,128)(2,1)}, bf16[1536,512]{1,0:T(8,128)(2,1)}, bf16[512,1536]{1,0:T(8,128)(2,1)}), ...) | async-done | bytes 7077904 | tf_op jit(solution)/shard_map/psum | solution.py:351
  (1991 shorter events, 1742.3 us)
Async XLA Ops:
  7.2 812.5 %copy-start = (bf16[512,1536]{1,0:T(8,128)(2,1)S(1)}, bf16[512,1536]{1,0:T(8,128)(2,1)}, u32[]{:S(2)}) copy-start(bf16[512,1536]{1,0:T(8,128)(2,1)} %param.30) | copy-start | bytes 4718596
  7.2 134.9 %copy-start.64 = (f32[1536]{0:T(1024)S(1)}, f32[1536]{0:T(1024)}, u32[]{:S(2)}) copy-start(f32[1536]{0:T(1024)} %param.25) | copy-start | bytes 18436
  7.2 134.8 %all-gather.5.cloned.1.call-start = ((), (), s32[]{:S(2)}) async-start(), calls=%async_computation.4 | async-start | bytes 15925248 | tf_op jit(solution)/shard_map/all_gather | solution.py:209
  8.0 634.8 %all-gather.7.cloned.1.call-start = ((), (), s32[]{:S(2)}) async-start(), calls=%async_computation.5 | async-start | bytes 5308416 | tf_op jit(solution)/shard_map/all_gather | solution.py:210
  9.3 142.0 %copy-start.72 = (f32[256]{0:T(256)}, f32[256]{0:T(256)S(1)}, u32[]{:S(2)}) copy-start(f32[256]{0:T(256)S(1)} %get-tuple-element.869) | copy-start | bytes 3076
  154.1 24.5 collective-permute-start.2
  157.4 61.1 %collective-permute-start.1 = (bf16[256,3072]{1,0:T(8,128)(2,1)}, bf16[256,3072]{1,0:T(8,128)(2,1)}, u32[]{:S(2)}, u32[]{:S(2)}) collective-permute-start(bf16[256,3072]{1,0:T(8,128)(2,1)} %slice.2477), channel_id=1, source_target_pairs={{0,2},{1,3},{2,4},{3,5},{4,6},{5,7},{8,10},{9,11},{10,12},{11,13},... | collective-permute-start | bytes 4718600 | tf_op jit(solution)/shard_map/ppermute | solution.py:14
  159.8 105.6 %collective-permute-start = (bf16[256,3072]{1,0:T(8,128)(2,1)}, bf16[256,3072]{1,0:T(8,128)(2,1)}, u32[]{:S(2)}, u32[]{:S(2)}) collective-permute-start(bf16[256,3072]{1,0:T(8,128)(2,1)} %slice.2477), channel_id=1, source_target_pairs={{0,3},{1,4},{2,5},{3,6},{4,7},{8,11},{9,12},{10,13},{11,14},{12,15... | collective-permute-start | bytes 4718600 | tf_op jit(solution)/shard_map/ppermute | solution.py:14
  162.3 591.8 %all-gather.9.cloned.1.call-start = ((), (), s32[]{:S(2)}) async-start(), calls=%async_computation.6 | async-start | bytes 7077888 | tf_op jit(solution)/shard_map/all_gather | solution.py:255
  165.4 3.6 collective-permute-start.3
  649.5 170.1 %all-gather.11.cloned.1.call-start = ((), (), s32[]{:S(2)}) async-start(), calls=%async_computation.8 | async-start | bytes 7077888 | tf_op jit(solution)/shard_map/all_gather | solution.py:266
  651.8 258.2 %reduce-scatter.7.cloned.1.call-start = ((), (), s32[]{:S(2)}) async-start(), calls=%async_computation.9 | async-start | bytes 7077888 | tf_op jit(solution)/shard_map/reduce_scatter | solution.py:280
  841.4 139.0 %reduce-scatter.5.cloned.1.call-start = ((), (), s32[]{:S(2)}) async-start(), calls=%async_computation.7 | async-start | bytes 7077888 | tf_op jit(solution)/shard_map/reduce_scatter | solution.py:259
  848.4 61.6 %copy-start.12 = (f32[256,1536]{1,0:T(8,128)S(1)}, f32[256,1536]{1,0:T(8,128)}, u32[]{:S(2)}) copy-start(f32[256,1536]{1,0:T(8,128)} %copy-done.11) | copy-start | bytes 4718596
  848.4 2844.7 %reduce-scatter.11.cloned.1.call-start = ((), (), s32[]{:S(2)}) async-start(), calls=%async_computation.11 | async-start | bytes 5308416 | tf_op jit(solution)/shard_map/reduce_scatter | solution.py:342
  1008.2 2832.7 %reduce-scatter.9.cloned.1.call-start = ((), (), s32[]{:S(2)}) async-start(), calls=%async_computation.10 | async-start | bytes 15925248 | tf_op jit(solution)/shard_map/reduce_scatter | solution.py:339
  1287.9 50.7 %copy-start.68 = (f32[2]{0:T(128)S(1)}, f32[2]{0:T(128)}, u32[]{:S(2)}) copy-start(f32[2]{0:T(128)} %get-tuple-element.1468) | copy-start | bytes 28 | tf_op jit(solution)/shard_map/while
  1603.2 50.7 %copy-start.68 = (f32[2]{0:T(128)S(1)}, f32[2]{0:T(128)}, u32[]{:S(2)}) copy-start(f32[2]{0:T(128)} %get-tuple-element.1468) | copy-start | bytes 28 | tf_op jit(solution)/shard_map/while
  1918.5 50.7 %copy-start.68 = (f32[2]{0:T(128)S(1)}, f32[2]{0:T(128)}, u32[]{:S(2)}) copy-start(f32[2]{0:T(128)} %get-tuple-element.1468) | copy-start | bytes 28 | tf_op jit(solution)/shard_map/while
  2233.7 50.7 %copy-start.68 = (f32[2]{0:T(128)S(1)}, f32[2]{0:T(128)}, u32[]{:S(2)}) copy-start(f32[2]{0:T(128)} %get-tuple-element.1468) | copy-start | bytes 28 | tf_op jit(solution)/shard_map/while
  2864.2 50.7 %copy-start.68 = (f32[2]{0:T(128)S(1)}, f32[2]{0:T(128)}, u32[]{:S(2)}) copy-start(f32[2]{0:T(128)} %get-tuple-element.1468) | copy-start | bytes 28 | tf_op jit(solution)/shard_map/while
  3179.5 50.7 %copy-start.68 = (f32[2]{0:T(128)S(1)}, f32[2]{0:T(128)}, u32[]{:S(2)}) copy-start(f32[2]{0:T(128)} %get-tuple-element.1468) | copy-start | bytes 28 | tf_op jit(solution)/shard_map/while
  3579.2 12.6 collective-permute-start.5
  3580.5 40.1 collective-permute-start.7
  3581.8 77.6 %collective-permute-start.6 = (bf16[256,3072]{0,1:T(8,128)(2,1)}, bf16[256,3072]{0,1:T(8,128)(2,1)}, u32[]{:S(2)}, u32[]{:S(2)}) collective-permute-start(bf16[256,3072]{0,1:T(8,128)(2,1)} %get-tuple-element.859), channel_id=1, source_target_pairs={{2,0},{3,1},{4,2},{5,3},{6,4},{7,5},{10,8},{11,9},{12,10},{13,11},... | collective-permute-start | bytes 4718600 | tf_op jit(solution)/shard_map/ppermute | solution.py:14
  3587.7 3.8 collective-permute-start.4
  3591.7 71.6 %copy-start.15 = (bf16[1,256,1536]{2,1,0:T(8,128)(2,1)S(1)}, bf16[1,256,1536]{2,1,0:T(8,128)(2,1)}, u32[]{:S(2)}) copy-start(bf16[1,256,1536]{2,1,0:T(8,128)(2,1)} %param.18) | copy-start | bytes 2359300
  3591.8 71.5 %copy-start.20 = (bf16[251,8,2,96]{0,3,2,1:T(8,128)(2,1)S(1)}, bf16[251,8,2,96]{0,3,2,1:T(8,128)(2,1)}, u32[]{:S(2)}) copy-start(bf16[251,8,2,96]{0,3,2,1:T(8,128)(2,1)} %slice.3701) | copy-start | bytes 2313220
  3591.8 71.5 %copy-start.65 = (f32[1536]{0:T(1024)S(1)}, f32[1536]{0:T(1024)}, u32[]{:S(2)}) copy-start(f32[1536]{0:T(1024)} %param.25) | copy-start | bytes 18436
  3591.8 71.5 %copy-start.73 = (f32[256]{0:T(256)S(1)}, f32[256]{0:T(256)}, u32[]{:S(2)}) copy-start(f32[256]{0:T(256)} %copy-done.72) | copy-start | bytes 3076
  3672.5 326.4 %all-reduce.6.cloned.1.call-start = ((), (), s32[]{:S(2)}) async-start(), calls=%async_computation.12 | async-start | bytes 14155776 | tf_op jit(solution)/shard_map/psum | solution.py:351
  3842.2 53.1 %copy-start.8 = (f32[256,1536]{1,0:T(8,128)S(1)}, f32[256,1536]{1,0:T(8,128)}, u32[]{:S(2)}) copy-start(f32[256,1536]{1,0:T(8,128)} %copy-done.7) | copy-start | bytes 4718596
  (409 other events, 3679.9 us)
Sparse Core Ops, SparseCore 0:
  9.7 132.3 all-gather.4
  162.4 82.5 all-gather.6
  649.7 104.4 all-gather.8
  756.2 63.4 all-gather.10
  841.5 68.4 reduce-scatter.6
  912.1 68.1 reduce-scatter.4
  1008.3 53.3 reduce-scatter.10
  3672.7 168.1 reduce-scatter.8
  3846.3 152.5 all-reduce.5
where the time goes:
time: 4040 us; the launch traced here: 4020 us
  other arithmetic  2010 us (50%)
  local copies, waits for them, and re-layouts  853 us (21%)
  waiting for transfers between devices  821 us (20%)
  matrix products  225 us (6%)
    mul x8, other arithmetic, attend_group_back(): dlogits = convolve_back(dconv, kernel_g) * mask_ext * score_scale  997 us
    another operation x576, local copies, waits for them, and re-layouts, kernel_grads(): entries.append(jnp.stack(line_sums, axis=-1))  678 us
    reduce_sum x32, other arithmetic, kernel_grads(): line_sums.append(jnp.sum(grads * window_part, axis=(1, 2)))  334 us
    reduce_sum x8, other arithmetic, attend_group_back(): dconv = prob * (dprob - jnp.sum(prob * dprob, axis=-1, keepdims=True))  294 us
    reduce_max x8, other arithmetic, attend_group(): peak = jnp.max(jnp.where(allowed, conv, -1e+30), axis=-1, keepdims=True)  277 us
    ppermute x8, waiting for transfers between devices, from_behind(): return lax.ppermute(x, axis, pairs)  155 us
    reduce_scatter x1, waiting for transfers between devices, on_device(): lax.psum_scatter(whole_input_grad.astype(jnp.bfloat16), 'seq', scatter_di...  148 us
    all_gather x1, waiting for transfers between devices, on_device(): lax.all_gather(input_weight, 'seq', axis=0, tiled=True)  133 us
  transfers between devices with their start and end apart: 17, of which 12 were waited for; matrix products, arithmetic and copies ran while one was open for 74% of the time, Pallas kernels for 0%

commit v1 on v0

--- a/solution.py
+++ b/solution.py
@@ -6,6 +6,18 @@
 REACH = 4
 EPS = 1e-06
 HIGHEST = lax.Precision.HIGHEST
+
+
+def gather_by_bits(array, axis, dim):
+    ways, here, lap = (lax.axis_size(axis), lax.axis_index(axis), array.shape[dim])
+    line, have = (array, 1)
+    while have < ways:
+        line = jnp.concatenate(
+            [line, lax.ppermute(line, axis, [(d, (d - have) % ways) for d in range(ways)])],
+            axis=dim,
+        )
+        have = 2 * have
+    return jnp.roll(line, here * lap, axis=dim)
 
 
 def from_behind(x, axis, by):
@@ -252,7 +264,7 @@
     normed_mid = (resid * second_scale * second_gain).astype(jnp.bfloat16)
     dmlp = (row_valid * grad_out).astype(jnp.bfloat16)
     contract_rows = (((0,), (0,)), ((), ()))
-    inputs_all = lax.all_gather(normed_mid, "seq", axis=0, tiled=True)
+    inputs_all = gather_by_bits(normed_mid, "seq", 0)
     gate = jnp.dot(inputs_all, gate_weight, preferred_element_type=jnp.float32)
     up_proj = jnp.dot(inputs_all, up_weight, preferred_element_type=jnp.float32)
     hidden = (jax.nn.silu(gate) * up_proj).astype(jnp.bfloat16)

time: 4040 us -> 3090 us (0.76)
  other arithmetic: 2010 us -> 1370 us
  local copies, waits for them, and re-layouts: 853 us -> 441 us
  waiting for transfers between devices: 821 us -> 893 us
    mul x8, other arithmetic: 997 us -> 356 us  [attend_group_back(): dlogits = convolve_back(dconv, kernel_g) * mask_ext * score_scale]
    another operation x576, local copies, waits for them, and re-layouts: 678 us -> 235 us  [kernel_grads(): entries.append(jnp.stack(line_sums, axis=-1))]
    ppermute x0 -> x3, waiting for transfers between devices: none -> 210 us  [gather_by_bits(): lax.ppermute(line, axis, [(d, (d - have) % ways) for d in range(ways)])]
    all_gather x1 -> x0, waiting for transfers between devices: 102 us -> none  [on_device(): inputs_all = lax.all_gather(normed_mid, 'seq', axis=0, tiled=True)]
    all_gather x1, waiting for transfers between devices: 51.8 us -> 0.01 us  [on_device(): dmlp_all = lax.all_gather(dmlp, 'seq', axis=0, tiled=True)]
  transfers between devices with their start and end apart: 17 -> 19, of which waited for: 12 -> 13; matrix products, arithmetic and copies ran while one was open for 74% -> 64% of each run, Pallas kernels for 0% -> 0%
where the time goes in v1:
time: 3090 us; the launch traced here: 3070 us
  other arithmetic  1370 us (44%)
  waiting for transfers between devices  893 us (29%)
  local copies, waits for them, and re-layouts  441 us (14%)
  matrix products  249 us (8%)
  starting transfers between devices  46.1 us (1%)
  blocking collectives  40.1 us (1%)
    mul x8, other arithmetic, attend_group_back(): dlogits = convolve_back(dconv, kernel_g) * mask_ext * score_scale  356 us
    reduce_sum x32, other arithmetic, kernel_grads(): line_sums.append(jnp.sum(grads * window_part, axis=(1, 2)))  335 us
    reduce_sum x8, other arithmetic, attend_group_back(): dconv = prob * (dprob - jnp.sum(prob * dprob, axis=-1, keepdims=True))  294 us
    reduce_max x8, other arithmetic, attend_group(): peak = jnp.max(jnp.where(allowed, conv, -1e+30), axis=-1, keepdims=True)  277 us
    another operation x576, local copies, waits for them, and re-layouts, kernel_grads(): entries.append(jnp.stack(line_sums, axis=-1))  235 us
    ppermute x3, waiting for transfers between devices, gather_by_bits(): lax.ppermute(line, axis, [(d, (d - have) % ways) for d in range(ways)])  210 us
    ppermute x8, waiting for transfers between devices, from_behind(): return lax.ppermute(x, axis, pairs)  176 us
    reduce_scatter x1, waiting for transfers between devices, on_device(): lax.psum_scatter(whole_input_grad.astype(jnp.bfloat16), 'seq', scatter_di...  139 us
  transfers between devices with their start and end apart: 19, of which 13 were waited for; matrix products, arithmetic and copies ran while one was open for 64% of the time, Pallas kernels for 0%

profile of v1, /device:TPU:0, one launch (start us, length us, event | category | flops | bytes accessed | tf_op | source)
XLA Modules:
  0.0 3073.3 jit_solution(1893872459746331300)
XLA Ops:
  9.7 132.4 %all-gather.4.cloned.1.call-done = bf16[1536,4608]{1,0:T(8,128)(2,1)} async-done(((bf16[192,4608]{1,0:T(8,128)(2,1)}), bf16[1536,4608]{1,0:T(8,128)(2,1)}) %all-gather.4.cloned.1.call-update) | async-done | bytes 14155792 | tf_op jit(solution)/shard_map/all_gather | solution.py:221
  175.4 46.4 %collective-permute-done = bf16[256,3072]{1,0:T(8,128)(2,1)} collective-permute-done((bf16[256,3072]{1,0:T(8,128)(2,1)}, bf16[256,3072]{1,0:T(8,128)(2,1)}, u32[]{:S(2)}, u32[]{:S(2)}) %collective-permute-start) | collective-permute-done | bytes 1572896 | tf_op jit(solution)/shard_map/ppermute | solution.py:26
  221.8 54.2 %collective-permute-done.1 = bf16[256,3072]{1,0:T(8,128)(2,1)} collective-permute-done((bf16[256,3072]{1,0:T(8,128)(2,1)}, bf16[256,3072]{1,0:T(8,128)(2,1)}, u32[]{:S(2)}, u32[]{:S(2)}) %collective-permute-start.1) | collective-permute-done | bytes 1572896 | tf_op jit(solution)/shard_map/ppermute | solution.py:26
  297.7 337.3 %while.34 = (s32[]{:T(128)}, f32[8,256,2,96]{1,3,2,0:T(8,128)}, f32[8,2,256,1]{2,1,3,0:T(2,128)}, bf16[8,1024,2,96]{1,3,2,0:T(8,128)(2,1)}, f32[8,2,2]{2,1,0:T(2...) while((s32[]{:T(128)}, f32[8,256,2,96]{1,3,2,0:T(8,128)}, ...), condition=%wide.region_4.5_spmd.clone, body=%wide.region_1.4_spmd.clone.sunk | while | flops 281692032 | bytes 160720112 | solution.py:250
  300.7 34.6 %select_reduce_fusion.2 = (f32[2,256]{1,0:T(2,128)S(1)}, f32[2,256,1024]{2,1,0:T(8,128)S(1)}) fusion(pred[256,1024]{1,0:T(8,128)(4,1)S(1)} %broadcast_compare_fusion.5, f32[2,261,1034]{2,1,0:T(8,128)S(1)} %convolution_multiply_fusion.5, f32[2]{0:T(128)S(1)} %get-tuple-element.1302, f32[2]{0:T(128)S(1)} %get-tuple-element.1303, ...), kind=kLoop, calls=%fused_computation.136.clone.1 | loop fusion | flops 69729792 | bytes 140773904 | tf_op jit(solution)/shard_map/while/body/eval_jaxpr/reduce_max | solution.py:91
  342.8 34.6 %select_reduce_fusion.2 = (f32[2,256]{1,0:T(2,128)S(1)}, f32[2,256,1024]{2,1,0:T(8,128)S(1)}) fusion(pred[256,1024]{1,0:T(8,128)(4,1)S(1)} %broadcast_compare_fusion.5, f32[2,261,1034]{2,1,0:T(8,128)S(1)} %convolution_multiply_fusion.5, f32[2]{0:T(128)S(1)} %get-tuple-element.1302, f32[2]{0:T(128)S(1)} %get-tuple-element.1303, ...), kind=kLoop, calls=%fused_computation.136.clone.1 | loop fusion | flops 69729792 | bytes 140773904 | tf_op jit(solution)/shard_map/while/body/eval_jaxpr/reduce_max | solution.py:91
  384.9 34.6 %select_reduce_fusion.2 = (f32[2,256]{1,0:T(2,128)S(1)}, f32[2,256,1024]{2,1,0:T(8,128)S(1)}) fusion(pred[256,1024]{1,0:T(8,128)(4,1)S(1)} %broadcast_compare_fusion.5, f32[2,261,1034]{2,1,0:T(8,128)S(1)} %convolution_multiply_fusion.5, f32[2]{0:T(128)S(1)} %get-tuple-element.1302, f32[2]{0:T(128)S(1)} %get-tuple-element.1303, ...), kind=kLoop, calls=%fused_computation.136.clone.1 | loop fusion | flops 69729792 | bytes 140773904 | tf_op jit(solution)/shard_map/while/body/eval_jaxpr/reduce_max | solution.py:91
  660.1 53.8 %collective-permute-done.4 = bf16[256,1536]{1,0:T(8,128)(2,1)S(1)} collective-permute-done((bf16[256,1536]{1,0:T(8,128)(2,1)S(1)}, bf16[256,1536]{1,0:T(8,128)(2,1)S(1)}, u32[]{:S(2)}, u32[]{:S(2)}) %collective-permute-start.4) | collective-permute-done | bytes 786464 | tf_op jit(solution)/shard_map/ppermute | solution.py:16
  789.2 124.2 %collective-permute-done.6 = bf16[1024,1536]{1,0:T(8,128)(2,1)} collective-permute-done((bf16[1024,1536]{1,0:T(8,128)(2,1)}, bf16[1024,1536]{1,0:T(8,128)(2,1)}, u32[]{:S(2)}, u32[]{:S(2)}) %collective-permute-start.6) | collective-permute-done | bytes 3145760 | tf_op jit(solution)/shard_map/ppermute | solution.py:16
  965.1 62.6 %reduce-scatter.7.cloned.1.call-done = bf16[256,1536]{1,0:T(8,128)(2,1)} async-done(((bf16[2048,1536]{1,0:T(8,128)(2,1)}), bf16[256,1536]{1,0:T(8,128)(2,1)}) %reduce-scatter.7.cloned.1.call-update) | async-done | bytes 786448 | tf_op jit(solution)/shard_map/reduce_scatter | solution.py:292
  1029.9 68.2 %reduce-scatter.5.cloned.1.call-done = bf16[256,1536]{1,0:T(8,128)(2,1)} async-done(((bf16[2048,1536]{1,0:T(8,128)(2,1)}), bf16[256,1536]{1,0:T(8,128)(2,1)}) %reduce-scatter.5.cloned.1.call-update) | async-done | bytes 786448 | tf_op jit(solution)/shard_map/reduce_scatter | solution.py:271
  1126.5 1489.3 %while.35 = (s32[]{:T(128)}, f32[8,261,2,96]{3,1,2,0:T(8,128)}, f32[8,1034,2,96]{1,3,2,0:T(8,128)}, f32[8,1024,2,96]{1,3,2,0:T(8,128)}, f32[8,2,6,11]{3,1,0,2:T(...) while((s32[]{:T(128)}, f32[8,261,2,96]{3,1,2,0:T(8,128)}, ...), condition=%wide.region_83.84_spmd.clone, body=%wide.region_13.83_spmd.clone.sunk | while | flops 1772737280 | bytes 377415552 | solution.py:316
  1137.6 36.7 %multiply_reduce_fusion.77 = (f32[2,256]{1,0:T(2,128)S(1)}, f32[2,256,1024]{2,1,0:T(8,128)S(1)}) fusion(f32[256,1024]{1,0:T(8,128)} %get-tuple-element.1394, f32[2]{0:T(128)} %get-tuple-element.1395, f32[256,1024]{1,0:T(8,128)S(1)} %get-tuple-element.1396, f32[2]{0:T(128)} %get-tuple-element.1397, f32[2,256]{1,0:T(2,128)S(1)} %fusion.372, ...), kind=kLoop, calls=%fused_computation.507.clone.1 | loop fusion | flops 72351232 | bytes 142873120 | tf_op jit(solution)/shard_map/while/body/eval_jaxpr/reduce_sum | solution.py:131
  1260.2 44.5 %multiply_multiply_fusion.4 = f32[2,261,1034]{2,1,0:T(8,128)} fusion(f32[2,256,1024]{2,1,0:T(8,128)S(1)} %copy-done.2, f32[261,1034]{1,0:T(8,128)} %fusion.373, f32[2]{0:T(128)S(1)} %get-tuple-element.1398, f32[2]{0:T(128)S(1)} %get-tuple-element.1399, f32[2]{0:T(128)S(1)} %get-tuple-element.1400, f32[2]{0:T(128)S(1)} %get-tuple-element.1401, ...), kind=kLoop, calls=%fused_computation.436.clone.1 | loop fusion | flops 71786448 | bytes 5336168 | tf_op jit(solution)/shard_map/while/body/eval_jaxpr/mul | solution.py:133
  1322.8 36.7 %multiply_reduce_fusion.77 = (f32[2,256]{1,0:T(2,128)S(1)}, f32[2,256,1024]{2,1,0:T(8,128)S(1)}) fusion(f32[256,1024]{1,0:T(8,128)} %get-tuple-element.1394, f32[2]{0:T(128)} %get-tuple-element.1395, f32[256,1024]{1,0:T(8,128)S(1)} %get-tuple-element.1396, f32[2]{0:T(128)} %get-tuple-element.1397, f32[2,256]{1,0:T(2,128)S(1)} %fusion.372, ...), kind=kLoop, calls=%fused_computation.507.clone.1 | loop fusion | flops 72351232 | bytes 142873120 | tf_op jit(solution)/shard_map/while/body/eval_jaxpr/reduce_sum | solution.py:131
  1445.3 44.5 %multiply_multiply_fusion.4 = f32[2,261,1034]{2,1,0:T(8,128)} fusion(f32[2,256,1024]{2,1,0:T(8,128)S(1)} %copy-done.2, f32[261,1034]{1,0:T(8,128)} %fusion.373, f32[2]{0:T(128)S(1)} %get-tuple-element.1398, f32[2]{0:T(128)S(1)} %get-tuple-element.1399, f32[2]{0:T(128)S(1)} %get-tuple-element.1400, f32[2]{0:T(128)S(1)} %get-tuple-element.1401, ...), kind=kLoop, calls=%fused_computation.436.clone.1 | loop fusion | flops 71786448 | bytes 5336168 | tf_op jit(solution)/shard_map/while/body/eval_jaxpr/mul | solution.py:133
  1508.0 36.7 %multiply_reduce_fusion.77 = (f32[2,256]{1,0:T(2,128)S(1)}, f32[2,256,1024]{2,1,0:T(8,128)S(1)}) fusion(f32[256,1024]{1,0:T(8,128)} %get-tuple-element.1394, f32[2]{0:T(128)} %get-tuple-element.1395, f32[256,1024]{1,0:T(8,128)S(1)} %get-tuple-element.1396, f32[2]{0:T(128)} %get-tuple-element.1397, f32[2,256]{1,0:T(2,128)S(1)} %fusion.372, ...), kind=kLoop, calls=%fused_computation.507.clone.1 | loop fusion | flops 72351232 | bytes 142873120 | tf_op jit(solution)/shard_map/while/body/eval_jaxpr/reduce_sum | solution.py:131
  1630.5 44.5 %multiply_multiply_fusion.4 = f32[2,261,1034]{2,1,0:T(8,128)} fusion(f32[2,256,1024]{2,1,0:T(8,128)S(1)} %copy-done.2, f32[261,1034]{1,0:T(8,128)} %fusion.373, f32[2]{0:T(128)S(1)} %get-tuple-element.1398, f32[2]{0:T(128)S(1)} %get-tuple-element.1399, f32[2]{0:T(128)S(1)} %get-tuple-element.1400, f32[2]{0:T(128)S(1)} %get-tuple-element.1401, ...), kind=kLoop, calls=%fused_computation.436.clone.1 | loop fusion | flops 71786448 | bytes 5336168 | tf_op jit(solution)/shard_map/while/body/eval_jaxpr/mul | solution.py:133
  1693.2 36.7 %multiply_reduce_fusion.77 = (f32[2,256]{1,0:T(2,128)S(1)}, f32[2,256,1024]{2,1,0:T(8,128)S(1)}) fusion(f32[256,1024]{1,0:T(8,128)} %get-tuple-element.1394, f32[2]{0:T(128)} %get-tuple-element.1395, f32[256,1024]{1,0:T(8,128)S(1)} %get-tuple-element.1396, f32[2]{0:T(128)} %get-tuple-element.1397, f32[2,256]{1,0:T(2,128)S(1)} %fusion.372, ...), kind=kLoop, calls=%fused_computation.507.clone.1 | loop fusion | flops 72351232 | bytes 142873120 | tf_op jit(solution)/shard_map/while/body/eval_jaxpr/reduce_sum | solution.py:131
  1815.7 44.5 %multiply_multiply_fusion.4 = f32[2,261,1034]{2,1,0:T(8,128)} fusion(f32[2,256,1024]{2,1,0:T(8,128)S(1)} %copy-done.2, f32[261,1034]{1,0:T(8,128)} %fusion.373, f32[2]{0:T(128)S(1)} %get-tuple-element.1398, f32[2]{0:T(128)S(1)} %get-tuple-element.1399, f32[2]{0:T(128)S(1)} %get-tuple-element.1400, f32[2]{0:T(128)S(1)} %get-tuple-element.1401, ...), kind=kLoop, calls=%fused_computation.436.clone.1 | loop fusion | flops 71786448 | bytes 5336168 | tf_op jit(solution)/shard_map/while/body/eval_jaxpr/mul | solution.py:133
  1878.3 36.7 %multiply_reduce_fusion.77 = (f32[2,256]{1,0:T(2,128)S(1)}, f32[2,256,1024]{2,1,0:T(8,128)S(1)}) fusion(f32[256,1024]{1,0:T(8,128)} %get-tuple-element.1394, f32[2]{0:T(128)} %get-tuple-element.1395, f32[256,1024]{1,0:T(8,128)S(1)} %get-tuple-element.1396, f32[2]{0:T(128)} %get-tuple-element.1397, f32[2,256]{1,0:T(2,128)S(1)} %fusion.372, ...), kind=kLoop, calls=%fused_computation.507.clone.1 | loop fusion | flops 72351232 | bytes 142873120 | tf_op jit(solution)/shard_map/while/body/eval_jaxpr/reduce_sum | solution.py:131
  2000.9 44.5 %multiply_multiply_fusion.4 = f32[2,261,1034]{2,1,0:T(8,128)} fusion(f32[2,256,1024]{2,1,0:T(8,128)S(1)} %copy-done.2, f32[261,1034]{1,0:T(8,128)} %fusion.373, f32[2]{0:T(128)S(1)} %get-tuple-element.1398, f32[2]{0:T(128)S(1)} %get-tuple-element.1399, f32[2]{0:T(128)S(1)} %get-tuple-element.1400, f32[2]{0:T(128)S(1)} %get-tuple-element.1401, ...), kind=kLoop, calls=%fused_computation.436.clone.1 | loop fusion | flops 71786448 | bytes 5336168 | tf_op jit(solution)/shard_map/while/body/eval_jaxpr/mul | solution.py:133
  2063.5 36.7 %multiply_reduce_fusion.77 = (f32[2,256]{1,0:T(2,128)S(1)}, f32[2,256,1024]{2,1,0:T(8,128)S(1)}) fusion(f32[256,1024]{1,0:T(8,128)} %get-tuple-element.1394, f32[2]{0:T(128)} %get-tuple-element.1395, f32[256,1024]{1,0:T(8,128)S(1)} %get-tuple-element.1396, f32[2]{0:T(128)} %get-tuple-element.1397, f32[2,256]{1,0:T(2,128)S(1)} %fusion.372, ...), kind=kLoop, calls=%fused_computation.507.clone.1 | loop fusion | flops 72351232 | bytes 142873120 | tf_op jit(solution)/shard_map/while/body/eval_jaxpr/reduce_sum | solution.py:131
  2186.1 44.5 %multiply_multiply_fusion.4 = f32[2,261,1034]{2,1,0:T(8,128)} fusion(f32[2,256,1024]{2,1,0:T(8,128)S(1)} %copy-done.2, f32[261,1034]{1,0:T(8,128)} %fusion.373, f32[2]{0:T(128)S(1)} %get-tuple-element.1398, f32[2]{0:T(128)S(1)} %get-tuple-element.1399, f32[2]{0:T(128)S(1)} %get-tuple-element.1400, f32[2]{0:T(128)S(1)} %get-tuple-element.1401, ...), kind=kLoop, calls=%fused_computation.436.clone.1 | loop fusion | flops 71786448 | bytes 5336168 | tf_op jit(solution)/shard_map/while/body/eval_jaxpr/mul | solution.py:133
  2248.7 36.7 %multiply_reduce_fusion.77 = (f32[2,256]{1,0:T(2,128)S(1)}, f32[2,256,1024]{2,1,0:T(8,128)S(1)}) fusion(f32[256,1024]{1,0:T(8,128)} %get-tuple-element.1394, f32[2]{0:T(128)} %get-tuple-element.1395, f32[256,1024]{1,0:T(8,128)S(1)} %get-tuple-element.1396, f32[2]{0:T(128)} %get-tuple-element.1397, f32[2,256]{1,0:T(2,128)S(1)} %fusion.372, ...), kind=kLoop, calls=%fused_computation.507.clone.1 | loop fusion | flops 72351232 | bytes 142873120 | tf_op jit(solution)/shard_map/while/body/eval_jaxpr/reduce_sum | solution.py:131
  2371.2 44.5 %multiply_multiply_fusion.4 = f32[2,261,1034]{2,1,0:T(8,128)} fusion(f32[2,256,1024]{2,1,0:T(8,128)S(1)} %copy-done.2, f32[261,1034]{1,0:T(8,128)} %fusion.373, f32[2]{0:T(128)S(1)} %get-tuple-element.1398, f32[2]{0:T(128)S(1)} %get-tuple-element.1399, f32[2]{0:T(128)S(1)} %get-tuple-element.1400, f32[2]{0:T(128)S(1)} %get-tuple-element.1401, ...), kind=kLoop, calls=%fused_computation.436.clone.1 | loop fusion | flops 71786448 | bytes 5336168 | tf_op jit(solution)/shard_map/while/body/eval_jaxpr/mul | solution.py:133
  2433.9 36.7 %multiply_reduce_fusion.77 = (f32[2,256]{1,0:T(2,128)S(1)}, f32[2,256,1024]{2,1,0:T(8,128)S(1)}) fusion(f32[256,1024]{1,0:T(8,128)} %get-tuple-element.1394, f32[2]{0:T(128)} %get-tuple-element.1395, f32[256,1024]{1,0:T(8,128)S(1)} %get-tuple-element.1396, f32[2]{0:T(128)} %get-tuple-element.1397, f32[2,256]{1,0:T(2,128)S(1)} %fusion.372, ...), kind=kLoop, calls=%fused_computation.507.clone.1 | loop fusion | flops 72351232 | bytes 142873120 | tf_op jit(solution)/shard_map/while/body/eval_jaxpr/reduce_sum | solution.py:131
  2556.4 44.5 %multiply_multiply_fusion.4 = f32[2,261,1034]{2,1,0:T(8,128)} fusion(f32[2,256,1024]{2,1,0:T(8,128)S(1)} %copy-done.2, f32[261,1034]{1,0:T(8,128)} %fusion.373, f32[2]{0:T(128)S(1)} %get-tuple-element.1398, f32[2]{0:T(128)S(1)} %get-tuple-element.1399, f32[2]{0:T(128)S(1)} %get-tuple-element.1400, f32[2]{0:T(128)S(1)} %get-tuple-element.1401, ...), kind=kLoop, calls=%fused_computation.436.clone.1 | loop fusion | flops 71786448 | bytes 5336168 | tf_op jit(solution)/shard_map/while/body/eval_jaxpr/mul | solution.py:133
  2649.2 41.8 %collective-permute-done.10 = bf16[256,3072]{0,1:T(8,128)(2,1)} collective-permute-done((bf16[256,3072]{0,1:T(8,128)(2,1)}, bf16[256,3072]{0,1:T(8,128)(2,1)}, u32[]{:S(2)}, u32[]{:S(2)}) %collective-permute-start.10) | collective-permute-done | bytes 1572896 | tf_op jit(solution)/shard_map/ppermute | solution.py:26
  2757.8 139.1 %reduce-scatter.9.cloned.1.call-done = bf16[192,4608]{1,0:T(8,128)(2,1)} async-done(((bf16[1536,4608]{1,0:T(8,128)(2,1)}), bf16[192,4608]{1,0:T(8,128)(2,1)}) %reduce-scatter.9.cloned.1.call-update) | async-done | bytes 1769488 | tf_op jit(solution)/shard_map/reduce_scatter | solution.py:351
  2908.7 40.1 %all-reduce.2 = (f32[16,6,11]{2,0,1:T(8,128)S(1)}, f32[8,2,2]{0,2,1:T(2,128)}, f32[1536]{0:T(1024)}, f32[1536]{0:T(1024)}, f32[1536]{0:T(1024)}) all-reduce(f32[16,6,11]{2,0,1:T(8,128)S(1)} %bitcast.778, f32[8,2,2]{0,2,1:T(2,128)S(1)} %copy.255, f32[1536]{0:T(1024)S(1)} %get-tuple-element.619, ...), channel_id=1, replica_groups=mesh['rep'=4,'seq'=8] {'rep','seq'}, use_global_device_ids=true, to_apply=%region_89.90 | all-reduce | flops 5696 | bytes 45568 | tf_op jit(solution)/shard_map/psum | solution.py:359
  2952.4 102.6 %all-reduce.6.cloned.1.call-done = (bf16[192,4608]{1,0:T(8,128)(2,1)}, bf16[192,1536]{1,0:T(8,128)(2,1)}, bf16[1536,512]{1,0:T(8,128)(2,1)}, bf16[1536,512]{1,0:T(8,128)(2,1)}, bf16[512,1536]{1,0:T(8,128)(2,1)}) async-done(((bf16[192,4608]{1,0:T(8,128)(2,1)}, bf16[192,1536]{1,0:T(8,128)(2,1)}, bf16[1536,512]{1,0:T(8,128)(2,1)}, bf16[1536,512]{1,0:T(8,128)(2,1)}, bf16[512,1536]{1,0:T(8,128)(2,1)}), ...) | async-done | bytes 7077904 | tf_op jit(solution)/shard_map/psum | solution.py:363
  (2726 shorter events, 1419.7 us)
Async XLA Ops:
  7.2 925.2 %copy-start = (bf16[1536,512]{1,0:T(8,128)(2,1)S(1)}, bf16[1536,512]{1,0:T(8,128)(2,1)}, u32[]{:S(2)}) copy-start(bf16[1536,512]{1,0:T(8,128)(2,1)} %param.28) | copy-start | bytes 4718596
  7.2 134.9 %copy-start.111 = (f32[1536]{0:T(1024)S(1)}, f32[1536]{0:T(1024)}, u32[]{:S(2)}) copy-start(f32[1536]{0:T(1024)} %param.25) | copy-start | bytes 18436
  7.2 134.8 %all-gather.4.cloned.1.call-start = ((), (), s32[]{:S(2)}) async-start(), calls=%async_computation.4 | async-start | bytes 15925248 | tf_op jit(solution)/shard_map/all_gather | solution.py:221
  8.0 646.5 %all-gather.6.cloned.1.call-start = ((), (), s32[]{:S(2)}) async-start(), calls=%async_computation.5 | async-start | bytes 5308416 | tf_op jit(solution)/shard_map/all_gather | solution.py:222
  8.7 768.8 %all-gather.8.cloned.1.call-start = ((), (), s32[]{:S(2)}) async-start(), calls=%async_computation.7 | async-start | bytes 7077888 | tf_op jit(solution)/shard_map/all_gather | solution.py:278
  9.7 141.6 %copy-start.119 = (f32[256]{0:T(256)}, f32[256]{0:T(256)S(1)}, u32[]{:S(2)}) copy-start(f32[256]{0:T(256)S(1)} %get-tuple-element.871) | copy-start | bytes 3076
  154.1 67.7 %collective-permute-start = (bf16[256,3072]{1,0:T(8,128)(2,1)}, bf16[256,3072]{1,0:T(8,128)(2,1)}, u32[]{:S(2)}, u32[]{:S(2)}) collective-permute-start(bf16[256,3072]{1,0:T(8,128)(2,1)} %slice.2477), channel_id=1, source_target_pairs={{0,3},{1,4},{2,5},{3,6},{4,7},{8,11},{9,12},{10,13},{11,14},{12,15... | collective-permute-start | bytes 4718600 | tf_op jit(solution)/shard_map/ppermute | solution.py:26
  156.7 119.3 %collective-permute-start.1 = (bf16[256,3072]{1,0:T(8,128)(2,1)}, bf16[256,3072]{1,0:T(8,128)(2,1)}, u32[]{:S(2)}, u32[]{:S(2)}) collective-permute-start(bf16[256,3072]{1,0:T(8,128)(2,1)} %slice.2477), channel_id=1, source_target_pairs={{0,2},{1,3},{2,4},{3,5},{4,6},{5,7},{8,10},{9,11},{10,12},{11,13},... | collective-permute-start | bytes 4718600 | tf_op jit(solution)/shard_map/ppermute | solution.py:26
  161.4 114.6 %collective-permute-start.2 = (bf16[256,3072]{1,0:T(8,128)(2,1)}, bf16[256,3072]{1,0:T(8,128)(2,1)}, u32[]{:S(2)}, u32[]{:S(2)}) collective-permute-start(bf16[256,3072]{1,0:T(8,128)(2,1)} %slice.2477), channel_id=1, source_target_pairs={{0,1},{1,2},{2,3},{3,4},{4,5},{5,6},{6,7},{8,9},{9,10},{10,11},{11... | collective-permute-start | bytes 4718600 | tf_op jit(solution)/shard_map/ppermute | solution.py:26
  165.1 862.6 %reduce-scatter.7.cloned.1.call-start = ((), (), s32[]{:S(2)}) async-start(), calls=%async_computation.8 | async-start | bytes 7077888 | tf_op jit(solution)/shard_map/reduce_scatter | solution.py:292
  166.7 4.2 collective-permute-start.3
  658.8 55.2 %copy-start.16 = (f32[256,1536]{1,0:T(8,128)}, f32[256,1536]{1,0:T(8,128)S(1)}, u32[]{:S(2)}) copy-start(f32[256,1536]{1,0:T(8,128)S(1)} %get-tuple-element.875) | copy-start | bytes 4718596
  660.1 53.8 %collective-permute-start.4 = (bf16[256,1536]{1,0:T(8,128)(2,1)S(1)}, bf16[256,1536]{1,0:T(8,128)(2,1)S(1)}, u32[]{:S(2)}, u32[]{:S(2)}) collective-permute-start(bf16[256,1536]{1,0:T(8,128)(2,1)S(1)} %get-tuple-element.713), channel_id=1, source_target_pairs={{0,7},{1,0},{2,1},{3,2},{4,3},{5,4},{6,5},{7,6},{8,15},{9,8},{10,9... | collective-permute-start | bytes 2359304 | tf_op jit(solution)/shard_map/ppermute | solution.py:16
  713.9 46.6 %copy-start.18 = (bf16[256,1536]{1,0:T(8,128)(2,1)}, bf16[256,1536]{1,0:T(8,128)(2,1)S(1)}, u32[]{:S(2)}) copy-start(bf16[256,1536]{1,0:T(8,128)(2,1)S(1)} %collective-permute-done.4) | copy-start | bytes 2359300
  714.0 44.5 %collective-permute-start.5 = (bf16[512,1536]{1,0:T(8,128)(2,1)S(1)}, bf16[512,1536]{1,0:T(8,128)(2,1)S(1)}, u32[]{:S(2)}, u32[]{:S(2)}) collective-permute-start(bf16[512,1536]{1,0:T(8,128)(2,1)S(1)} %pad_maximum_fusion.5), channel_id=1, source_target_pairs={{0,6},{1,7},{2,0},{3,1},{4,2},{5,3},{6,4},{7,5},{8,14},{9,15},{10,... | collective-permute-start | bytes 4718600 | tf_op jit(solution)/shard_map/ppermute | solution.py:16
  760.7 152.8 %collective-permute-start.6 = (bf16[1024,1536]{1,0:T(8,128)(2,1)}, bf16[1024,1536]{1,0:T(8,128)(2,1)}, u32[]{:S(2)}, u32[]{:S(2)}) collective-permute-start(bf16[1024,1536]{1,0:T(8,128)(2,1)} %pad_maximum_fusion.3), channel_id=1, source_target_pairs={{0,4},{1,5},{2,6},{3,7},{4,0},{5,1},{6,2},{7,3},{8,12},{9,13},{10,... | collective-permute-start | bytes 9437192 | tf_op jit(solution)/shard_map/ppermute | solution.py:16
  956.2 141.9 %reduce-scatter.5.cloned.1.call-start = ((), (), s32[]{:S(2)}) async-start(), calls=%async_computation.6 | async-start | bytes 7077888 | tf_op jit(solution)/shard_map/reduce_scatter | solution.py:271
  964.4 63.3 %copy-start.17 = (f32[256,1536]{1,0:T(8,128)S(1)}, f32[256,1536]{1,0:T(8,128)}, u32[]{:S(2)}) copy-start(f32[256,1536]{1,0:T(8,128)} %copy-done.16) | copy-start | bytes 4718596
  964.5 133.6 %copy-start.25 = (bf16[1,256,1536]{2,1,0:T(8,128)(2,1)S(1)}, bf16[1,256,1536]{2,1,0:T(8,128)(2,1)}, u32[]{:S(2)}) copy-start(bf16[1,256,1536]{2,1,0:T(8,128)(2,1)} %param.31) | copy-start | bytes 2359300
  964.5 1793.3 %reduce-scatter.11.cloned.1.call-start = ((), (), s32[]{:S(2)}) async-start(), calls=%async_computation.10 | async-start | bytes 5308416 | tf_op jit(solution)/shard_map/reduce_scatter | solution.py:354
  1126.4 1770.5 %reduce-scatter.9.cloned.1.call-start = ((), (), s32[]{:S(2)}) async-start(), calls=%async_computation.9 | async-start | bytes 15925248 | tf_op jit(solution)/shard_map/reduce_scatter | solution.py:351
  2635.9 55.1 %collective-permute-start.10 = (bf16[256,3072]{0,1:T(8,128)(2,1)}, bf16[256,3072]{0,1:T(8,128)(2,1)}, u32[]{:S(2)}, u32[]{:S(2)}) collective-permute-start(bf16[256,3072]{0,1:T(8,128)(2,1)} %get-tuple-element.860), channel_id=1, source_target_pairs={{3,0},{4,1},{5,2},{6,3},{7,4},{11,8},{12,9},{13,10},{14,11},{15,12... | collective-permute-start | bytes 4718600 | tf_op jit(solution)/shard_map/ppermute | solution.py:26
  2637.1 53.8 %collective-permute-start.8 = (bf16[256,3072]{0,1:T(8,128)(2,1)}, bf16[256,3072]{0,1:T(8,128)(2,1)}, u32[]{:S(2)}, u32[]{:S(2)}) collective-permute-start(bf16[256,3072]{0,1:T(8,128)(2,1)} %get-tuple-element.859), channel_id=1, source_target_pairs={{1,0},{2,1},{3,2},{4,3},{5,4},{6,5},{7,6},{9,8},{10,9},{11,10},{12... | collective-permute-start | bytes 4718600 | tf_op jit(solution)/shard_map/ppermute | solution.py:26
  2638.4 85.4 %collective-permute-start.9 = (bf16[256,3072]{0,1:T(8,128)(2,1)}, bf16[256,3072]{0,1:T(8,128)(2,1)}, u32[]{:S(2)}, u32[]{:S(2)}) collective-permute-start(bf16[256,3072]{0,1:T(8,128)(2,1)} %get-tuple-element.861), channel_id=1, source_target_pairs={{2,0},{3,1},{4,2},{5,3},{6,4},{7,5},{10,8},{11,9},{12,10},{13,11},... | collective-permute-start | bytes 4718600 | tf_op jit(solution)/shard_map/ppermute | solution.py:26
  2644.4 3.8 collective-permute-start.7
  2649.1 78.7 %copy-start.22 = (bf16[1,256,1536]{2,1,0:T(8,128)(2,1)S(1)}, bf16[1,256,1536]{2,1,0:T(8,128)(2,1)}, u32[]{:S(2)}) copy-start(bf16[1,256,1536]{2,1,0:T(8,128)(2,1)} %param.18) | copy-start | bytes 2359300
  2649.1 78.7 %copy-start.26 = (bf16[251,8,2,96]{0,3,2,1:T(8,128)(2,1)S(1)}, bf16[251,8,2,96]{0,3,2,1:T(8,128)(2,1)}, u32[]{:S(2)}) copy-start(bf16[251,8,2,96]{0,3,2,1:T(8,128)(2,1)} %slice.3701) | copy-start | bytes 2313220
  2649.2 78.7 %copy-start.112 = (f32[1536]{0:T(1024)S(1)}, f32[1536]{0:T(1024)}, u32[]{:S(2)}) copy-start(f32[1536]{0:T(1024)} %param.25) | copy-start | bytes 18436
  2649.2 78.8 %copy-start.120 = (f32[256]{0:T(256)S(1)}, f32[256]{0:T(256)}, u32[]{:S(2)}) copy-start(f32[256]{0:T(256)} %copy-done.119) | copy-start | bytes 3076
  2737.1 317.9 %all-reduce.6.cloned.1.call-start = ((), (), s32[]{:S(2)}) async-start(), calls=%async_computation.11 | async-start | bytes 14155776 | tf_op jit(solution)/shard_map/psum | solution.py:363
  2897.7 51.9 %copy-start.11 = (f32[256,1536]{1,0:T(8,128)S(1)}, f32[256,1536]{1,0:T(8,128)}, u32[]{:S(2)}) copy-start(f32[256,1536]{1,0:T(8,128)} %copy-done.10) | copy-start | bytes 4718596
  2897.7 51.9 %copy-start.131 = (f32[256]{0:T(256)S(1)}, f32[256]{0:T(256)}, u32[]{:S(2)}) copy-start(f32[256]{0:T(256)} %get-tuple-element.870) | copy-start | bytes 3076
  (772 other events, 5569.1 us)
Sparse Core Ops, SparseCore 0:
  9.7 132.3 all-gather.3
  143.7 75.9 all-gather.5
  221.9 99.1 all-gather.7
  956.3 71.3 reduce-scatter.6
  1029.8 68.1 reduce-scatter.4
  1126.5 53.3 reduce-scatter.10
  2737.2 159.6 reduce-scatter.8
  2902.3 152.6 all-reduce.5
